TPU v7x, 256 devices: a whole 4x4x8 slice. The times are simulated.
256 devices in a mesh: gx: 32 (over x, z_hi, y), vz: 8 (over z_lo, core).
Axes of the slice: x: 4, y: 4, z: 8 (z_hi: 2, z_lo: 4; z = z_hi * 4 + z_lo), core: 2. Of those that a mesh axis runs over, the one named last changes fastest.
Arguments:
- density: float32 [24, 256, 64, 256], P('vz', 'gx'), may hold values from 0.02 to 2.5, as said below
- shift_depth: int32 [16], replicated, may hold values from -20 to 20, as said below
- sub_cell: float32 [16], replicated, may hold values from 0 to 1
- gravity_kick: float32 [256, 64], P('gx'), may hold values from -0.9 to 0.9
- collision: float32 [256, 64], P('gx'), may hold values from 0.1 to 10
Outputs:
- relaxed: float32 [24, 256, 64, 256], P('vz', 'gx')
Inputs may be any that keep to these rules, and one draw needn't show every extreme that they name: `density`: every value is positive. `shift_depth`: some x velocity has 20 and some has -20.
All inputs are finite; a program needn't handle non-finite values.
Results may differ from a plain program's by a relative error of at most 0.00002.
Values sent between devices are 32-bit elements; how exact they have to be, the bound alone decides.
A program may use at most 64 MiB of HBM per device.

v0:
```python
import functools
import math

import jax
import jax.numpy as jnp
from jax import lax
from jax.experimental import pallas as pl
from jax.experimental.pallas import tpu as pltpu
from jax.sharding import Mesh
from jax.sharding import PartitionSpec as P

AXES = ("x", "zh", "y", "zl", "core")
VZ = ("zl", "core")
GX = ("x", "zh", "y")
MESH = pl.DeviceIdType.MESH
HIGH = lax.Precision.HIGHEST

NVX = 16
COLS = 8
WIDE = 32
ROWS = 64
QUARTER = 16
PLANES = 3
TOTAL_VZ = 24
TR = 8
TILES = QUARTER // TR
CHUNKS = [(p, t) for p in (0, 2, 1) for t in range(TILES)]
N = len(CHUNKS)
LENGTHS = (23, 25, 26, 28, 30, 33, 42)
REACH = 21
SPAN = WIDE + 2 * REACH

LANES = (slice(0, 128), slice(128, 256))
STEP_XY = 9.0 / 16
STEP_Z = 9.6 / TOTAL_VZ
CELL = STEP_XY * STEP_XY * STEP_Z


def places_of(depth):
    depths = [depth[i] for i in range(NVX)]
    counts = [jnp.where(d >= 0, d + 1, -d) for d in depths]
    ranks = [jnp.int32(0)] * NVX
    for i in range(NVX):
        for j in range(i):
            behind = (counts[i] <= counts[j]).astype(jnp.int32)
            ranks[i] = ranks[i] + behind
            ranks[j] = ranks[j] + 1 - behind
    return depths, counts, [jnp.where(r < 8, r, 23 - r) for r in ranks]


def kernel(
    cap,
    depth,
    sub,
    kick,
    rate,
    dens,
    kicked_out,
    coef,
    *scratch,
):
    scratch = list(scratch)
    take = lambda k: [scratch.pop(0) for _ in range(k)]
    block, packed, lists, chosen, moved = (take(N) for _ in range(5))
    planes, kick_wide, plane_sums, part, parts, kicked, order, local, remote_cols, mixed = take(10)
    y1_own, y1_out, y1_in, z_out, z_in, x_out, x_in = take(7)
    y2_own, y2_out, y2_in, halo_out, halo_in, sum_out, sum_in, kicked_sem = take(8)

    x, zh, y = (lax.axis_index(a) for a in GX)
    zl, core = (lax.axis_index(a) for a in VZ)
    nx = lax.axis_size("x")
    slab = zl * 2 + core
    slabs = lax.axis_size("zl") * 2

    def slab_device(v):
        return {"zl": v // 2, "core": v % 2}

    barrier = pltpu.get_barrier_semaphore()
    friends = [{"y": (y + k) % 4} for k in (1, 2, 3)]
    friends += [{"zh": 1 - zh}, {"x": (x + 1) % nx}, {"x": (x + nx - 1) % nx}]
    friends += [slab_device((slab + k) % slabs) for k in range(1, 8)]
    for friend in friends:
        pl.semaphore_signal(barrier, inc=1, device_id=friend, device_id_type=MESH)

    own = []
    for c, (p, t) in enumerate(CHUNKS):
        rows = pl.ds(y * QUARTER + t * TR, TR)
        own.append(pltpu.make_async_copy(dens.at[p, :, rows, :], block[c].at[pl.ds(y * COLS, COLS)], y1_own.at[c]))
        own[c].start()
    pl.semaphore_wait(barrier, len(friends))

    def remote(src, dst, send, recv, device):
        return pltpu.make_async_remote_copy(
            src_ref=src, dst_ref=dst, send_sem=send, recv_sem=recv, device_id=device, device_id_type=MESH
        )

    for c, (p, t) in enumerate(CHUNKS):
        for k in range(3):
            to = (y + k + 1) % 4
            rows = pl.ds(to * QUARTER + t * TR, TR)
            remote(
                dens.at[p, :, rows, :], block[c].at[pl.ds(y * COLS, COLS)], y1_out.at[c], y1_in.at[c], {"y": to}
            ).start()

    def three(ref, send, recv):
        part = ref.at[pl.ds(0, 3 * COLS)]
        return remote(part, part, send, recv, {"y": (y + 1) % 4})

    y1 = [three(block[c], y1_out.at[c], y1_in.at[c]) for c in range(N)]
    y2 = [three(moved[c], y2_out.at[c], y2_in.at[c]) for c in range(N)]

    depths, counts, places = places_of(depth)

    def at_place(values, q):
        acc = values[0]
        for i in range(1, NVX):
            acc = jnp.where(places[i] == q, values[i], acc)
        return acc

    depths = [at_place(depths, q) for q in range(NVX)]
    far = [at_place([sub[i] for i in range(NVX)], q) for q in range(NVX)]
    counts = [jnp.where(d >= 0, d + 1, -d) for d in depths]
    edge = [REACH + jnp.where(d >= 0, WIDE - 1 - d, 0) for d in depths]
    upper = edge[:8]
    lower = [SPAN + edge[8 + s] - counts[s] for s in range(8)]
    lists_at = [jnp.where(d >= 0, 0, cap - d - REACH) for d in depths]
    for s in range(8):
        lists_at[8 + s] = lists_at[8 + s] + counts[s]

    to_lane = lax.broadcasted_iota(jnp.int32, (16, 256), 1)
    to_sub = lax.broadcasted_iota(jnp.int32, (16, 256), 0)
    for i in range(NVX):
        order[i * 16 : i * 16 + 16, :] = (to_lane == places[i] * 16 + to_sub).astype(jnp.bfloat16)

    def permute(values, back):
        total = None
        for _ in range(3):
            piece = values.astype(jnp.bfloat16)
            values = values - piece.astype(jnp.float32)
            term = lax.dot_general(
                piece, order[...], (((1,), (1 if back else 0,)), ((), ())), preferred_element_type=jnp.float32
            )
            total = term if total is None else total + term
        return total

    lane_group = lax.broadcasted_iota(jnp.int32, (TR, 128), 1) >> 4

    def by_group(values, h):
        acc = jnp.full((TR, 128), values[h * 8])
        for s in range(1, 8):
            acc = jnp.where(lane_group == s, values[h * 8 + s], acc)
        return acc

    lane_depth = [by_group(depths, h) for h in range(2)]
    lane_far = [by_group(far, h) for h in range(2)]

    pair = lax.broadcasted_iota(jnp.int32, (8, 256), 1)
    vx_odd = (pair >> 4) * 2 - 15
    vy_odd = (pair & 15) * 2 - 15
    which = lax.broadcasted_iota(jnp.int32, (8, 256), 0)
    weights = (
        jnp.where(
            which == 0,
            1,
            jnp.where(
                which == 1, vx_odd, jnp.where(which == 2, vy_odd, jnp.where(which == 3, (vx_odd**2 + vy_odd**2) >> 1, 0))
            ),
        )
        .astype(jnp.float32)
        .astype(jnp.bfloat16)
    )

    def spread(values, c):
        pick = (lax.broadcasted_iota(jnp.int32, (8, 128), 0) == c).astype(jnp.float32)
        return lax.dot_general(
            values, pick, (((0,), (0,)), ((), ())), precision=HIGH, preferred_element_type=jnp.float32
        )

    def widen_kick(c, _):
        kick_wide[c] = spread(kick[...], c)
        return 0

    lax.fori_loop(0, COLS, widen_kick, 0)

    @pl.when(slab == 0)
    def _():
        planes[0] = jnp.zeros((COLS, ROWS, 256), jnp.float32)

    @pl.when(slab == slabs - 1)
    def _():
        planes[4] = jnp.zeros((COLS, ROWS, 256), jnp.float32)

    z_copies, x_copies, y2_self = {}, {}, {}
    pieces = [(c, 0, cap) for c in range(N - 1)] + [(N - 1, 0, cap // 2), (N - 1, cap // 2, cap)]

    def stage_pack(c):
        own[c].wait()
        y1[c].wait_recv()

        def line_up(b, _):
            cols = pl.ds(b * COLS, COLS)
            lined = permute(block[c][cols].reshape(COLS * TR, 256), False)
            for h in range(2):
                local[pl.ds(h * SPAN + REACH + b * COLS, COLS)] = lined[:, LANES[h]].reshape(COLS, TR, 128)
            return 0

        if c == 0:
            for b in range(4):
                line_up(b, 0)
        else:
            lax.fori_loop(0, 4, line_up, 0)

        def one_row(r, _):
            acc = None
            for s in range(8):
                piece = local[r + jnp.where(r < counts[s], upper[s], lower[s])]
                acc = piece if s == 0 else jnp.where(lane_group == s, piece, acc)
            packed[c][r] = acc
            return 0

        lax.fori_loop(0, cap, one_row, 0)
        for e, (q, low, high) in enumerate(pieces):
            if q == c:
                z_copies[e] = remote(
                    packed[c].at[pl.ds(low, high - low)],
                    lists[c].at[pl.ds(zh * cap + low, high - low)],
                    z_out.at[e],
                    z_in.at[e],
                    {"zh": 1 - zh},
                )
                z_copies[e].start()

        def one_col(n, _):
            for h in range(2):
                acc = None
                for s in range(8):
                    piece = local[n + (h * SPAN + REACH - 1 - depths[h * 8 + s])]
                    acc = piece if s == 0 else jnp.where(lane_group == s, piece, acc)
                chosen[c][n, :, LANES[h]] = acc
            return 0

        lax.fori_loop(0, WIDE + 1, one_col, 0)

    def stage_forward(e):
        c, low, high = pieces[e]
        z_copies[e].wait_recv()
        x_copies[e] = remote(
            lists[c].at[pl.ds((1 - zh) * cap + low, high - low)],
            lists[c].at[pl.ds(zh * cap + low, high - low)],
            x_out.at[e],
            x_in.at[e],
            {"x": (x + 1 - 2 * zh + nx) % nx},
        )
        x_copies[e].start()

    def stage_merge(c):
        for e, (q, _, _) in enumerate(pieces):
            if q == c:
                x_copies[e].wait_recv()
        p, t = CHUNKS[c]

        def one_remote(j, _):
            for h in range(2):
                acc = None
                for s in range(8):
                    piece = lists[c][j + lists_at[h * 8 + s]]
                    acc = piece if s == 0 else jnp.where(lane_group == s, piece, acc)
                remote_cols[j + 12, :, LANES[h]] = acc
            return 0

        lax.fori_loop(0, REACH, one_remote, 0)

        def column(n):
            got = []
            for h in range(2):
                from_col = n - 1 - lane_depth[h]
                inside = jnp.logical_and(from_col >= 0, from_col < WIDE)
                beyond = jnp.where(
                    lane_depth[h] >= 0, remote_cols[n + 12, :, LANES[h]], remote_cols[n, :, LANES[h]]
                )
                got.append(jnp.where(inside, chosen[c][n, :, LANES[h]], beyond))
            return got

        here = planes.at[p + 1, :, pl.ds(y * QUARTER + t * TR, TR), :]
        y2_self[c] = pltpu.make_async_copy(moved[c].at[pl.ds(y * COLS, COLS)], here, y2_own.at[c])

        def one_target(k, _):
            to = (y + k + 1) % 4

            def one_col(m, before):
                n = to * COLS + m
                now = column(n + 1)
                for h in range(2):
                    mixed[n, :, LANES[h]] = (1.0 - lane_far[h]) * now[h] + lane_far[h] * before[h]
                return tuple(now)

            lax.fori_loop(0, COLS, one_col, tuple(column(to * COLS)))
            cols = pl.ds(to * COLS, COLS)
            moved[c][cols] = permute(mixed[cols].reshape(COLS * TR, 256), True).reshape(COLS, TR, 256)

            @pl.when(k < 3)
            def _():
                remote(moved[c].at[cols], here, y2_out.at[c], y2_in.at[c], {"y": to}).start()

            return 0

        lax.fori_loop(0, 4, one_target, 0)
        y2_self[c].start()

    down = remote(planes.at[1], planes.at[4], halo_out.at[0], halo_in.at[0], slab_device((slab + slabs - 1) % slabs))
    up = remote(planes.at[3], planes.at[0], halo_out.at[1], halo_in.at[1], slab_device((slab + 1) % slabs))

    def stage_plane(p):
        for c, (q, _) in enumerate(CHUNKS):
            if q == p:
                y2_self[c].wait()
                y2[c].wait_recv()
        if p == 0:
            pl.when(slab > 0)(down.start)
        if p == 2:
            pl.when(slab < slabs - 1)(up.start)

        def four_cols(b, _):
            sums = None
            values = planes[p + 1, pl.ds(b * 4, 4)].reshape(4 * ROWS, 256)
            for _ in range(3):
                piece = values.astype(jnp.bfloat16)
                values = values - piece.astype(jnp.float32)
                term = lax.dot_general(weights, piece, (((1,), (1,)), ((), ())), preferred_element_type=jnp.float32)
                sums = term if sums is None else sums + term
            for c in range(4):
                plane_sums[p, b * 4 + c] = sums[:, c * ROWS : (c + 1) * ROWS]
            return 0

        for b in range(2):
            four_cols(b, 0)

    for name, c in ORDER:
        {"A": stage_pack, "B": stage_forward, "C": stage_merge, "D": stage_plane}[name](c)

    a = kick[...]
    lift, drop, stay = jnp.maximum(a, 0.0), jnp.maximum(-a, 0.0), 1.0 - jnp.abs(a)
    totals = [jnp.zeros((COLS, ROWS), jnp.float32) for _ in range(5)]
    for p in range(PLANES):
        level = slab * PLANES + p
        up_on = jnp.where(level + 1 < TOTAL_VZ, lift, 0.0)
        down_on = jnp.where(level >= 1, drop, 0.0)
        vz = (level.astype(jnp.float32) - 11.5) * STEP_Z
        above = ((level + 1).astype(jnp.float32) - 11.5) * STEP_Z
        below = ((level - 1).astype(jnp.float32) - 11.5) * STEP_Z
        kept = stay + up_on + down_on
        lean = stay * vz + up_on * above + down_on * below
        heat = stay * (vz * vz) + up_on * (above * above) + down_on * (below * below)
        n0, n1, n2, n3 = (
            unit * plane_sums[p, :, j, :] for j, unit in enumerate((1.0, STEP_XY / 2, STEP_XY / 2, STEP_XY**2 / 2))
        )
        for j, term in enumerate((n0 * kept, n1 * kept, n2 * kept, n0 * lean, n3 * kept + n0 * heat)):
            totals[j] = totals[j] + term
    for j in range(5):
        part[j // 2, :, j % 2 * ROWS : (j % 2 + 1) * ROWS] = totals[j]

    for k in range(7):
        remote(part, parts.at[k], sum_out, sum_in, slab_device((slab + k + 1) % slabs)).start()
    shares = remote(parts, parts, sum_out, sum_in, slab_device((slab + 1) % slabs))
    pl.when(slab > 0)(up.wait_recv)
    pl.when(slab < slabs - 1)(down.wait_recv)

    def kick_col(c, _):
        a = kick_wide[c]
        lift, drop, stay = jnp.maximum(a, 0.0), jnp.maximum(-a, 0.0), 1.0 - jnp.abs(a)
        for lanes in LANES:
            for p in range(PLANES):
                kicked[p, c, :, lanes] = (
                    stay * planes[p + 1, c, :, lanes] + lift * planes[p, c, :, lanes] + drop * planes[p + 2, c, :, lanes]
                )
        return 0

    lax.fori_loop(0, COLS, kick_col, 0)
    kicked_copy = pltpu.make_async_copy(kicked, kicked_out, kicked_sem)
    kicked_copy.start()

    shares.wait_recv()
    for j in range(5):
        for k in range(7):
            totals[j] = totals[j] + parts[k, j // 2, :, j % 2 * ROWS : (j % 2 + 1) * ROWS]

    mass = CELL * totals[0]
    flow_x = CELL * totals[1] / mass
    flow_y = CELL * totals[2] / mass
    flow_z = CELL * totals[3] / mass
    warm = (CELL * totals[4] - mass * (flow_x**2 + flow_y**2 + flow_z**2)) / (3.0 * mass)
    r = rate[...]
    share = 1.0 / (1.0 + r)
    two_pi_t = (2.0 * math.pi) * warm
    top = mass / (two_pi_t * jnp.sqrt(two_pi_t))
    for j, value in enumerate((share, r * share * top, -0.5 / warm, flow_x, flow_y, flow_z)):
        coef[j] = value

    kicked_copy.wait()
    pl.when(slab > 0)(down.wait_send)
    pl.when(slab < slabs - 1)(up.wait_send)
    shares.wait_send()
    for e in range(len(pieces)):
        z_copies[e].wait_send()
        x_copies[e].wait_send()
    for c in range(N):
        y1[c].wait_send()
        y2[c].wait_send()


ORDER = tuple(zip("AAAAAABBCBCBCBCBDBCCDD", (0, 1, 2, 3, 4, 5, 0, 1, 0, 2, 1, 3, 2, 4, 3, 5, 0, 6, 4, 5, 2, 1)))


def step(cap, collective_id, density, shift_depth, sub_cell, gravity_kick, collision):
    f32 = jnp.float32
    vmem = pl.BlockSpec(memory_space=pltpu.VMEM)
    smem = pl.BlockSpec(memory_space=pltpu.SMEM)
    dma = pltpu.SemaphoreType.DMA
    return pl.pallas_call(
        functools.partial(kernel, cap),
        out_shape=(
            jax.ShapeDtypeStruct((PLANES, COLS, ROWS, 256), f32),
            jax.ShapeDtypeStruct((6, COLS, ROWS), f32),
        ),
        in_specs=[smem, smem, vmem, vmem, pl.BlockSpec(memory_space=pl.ANY)],
        out_specs=(pl.BlockSpec(memory_space=pl.ANY), vmem),
        scratch_shapes=[pltpu.VMEM((WIDE, TR, 256), f32)] * N
        + [pltpu.VMEM((cap, TR, 128), f32)] * N
        + [pltpu.VMEM((max(2 * cap, cap + 2 * REACH), TR, 128), f32)] * N
        + [pltpu.VMEM((WIDE + 1, TR, 256), f32)] * N
        + [pltpu.VMEM((WIDE, TR, 256), f32)] * N
        + [
            pltpu.VMEM((5, COLS, ROWS, 256), f32),
            pltpu.VMEM((COLS, ROWS, 128), f32),
            pltpu.VMEM((PLANES, COLS, 8, ROWS), f32),
            pltpu.VMEM((3, COLS, 128), f32),
            pltpu.VMEM((7, 3, COLS, 128), f32),
            pltpu.VMEM((PLANES, COLS, ROWS, 256), f32),
            pltpu.VMEM((256, 256), jnp.bfloat16),
            pltpu.VMEM((2 * SPAN + 2 * REACH, TR, 128), f32),
            pltpu.VMEM((REACH + 24, TR, 256), f32),
            pltpu.VMEM((WIDE, TR, 256), f32),
            dma((N,)),
            dma((N,)),
            dma((N,)),
            dma((N + 1,)),
            dma((N + 1,)),
            dma((N + 1,)),
            dma((N + 1,)),
            dma((N,)),
            dma((N,)),
            dma((N,)),
            dma((2,)),
            dma((2,)),
            dma,
            dma,
            dma,
        ],
        compiler_params=pltpu.CompilerParams(collective_id=collective_id, has_side_effects=True),
    )(shift_depth, sub_cell, gravity_kick, collision, density)


def branch_kernel(depth, branch):
    _, counts, places = places_of(depth)
    need = jnp.int32(0)
    for i in range(NVX):
        for j in range(i):
            gap = places[i] - places[j]
            together = jnp.logical_or(gap == 8, gap == -8)
            need = jnp.maximum(need, jnp.where(together, counts[i] + counts[j], 0))
    k = jnp.int32(0)
    for rows in LENGTHS[:-1]:
        k = k + (need > rows).astype(jnp.int32)
    branch[0] = k


def per_device(density, shift_depth, sub_cell, gravity_kick, collision):
    branches = [functools.partial(step, rows, k + 1) for k, rows in enumerate(LENGTHS)]
    smem = pl.BlockSpec(memory_space=pltpu.SMEM)
    branch = pl.pallas_call(
        branch_kernel, out_shape=jax.ShapeDtypeStruct((1,), jnp.int32), in_specs=[smem], out_specs=smem
    )(shift_depth)[0]
    kicked, coef = lax.switch(branch, branches, density, shift_depth, sub_cell, gravity_kick, collision)
    keep, gain, cool, flow_x, flow_y, flow_z = (coef[j][:, :, None] for j in range(6))
    pair = jnp.arange(256, dtype=jnp.int32)
    vx = ((pair >> 4).astype(jnp.float32) - 7.5) * STEP_XY
    vy = ((pair & 15).astype(jnp.float32) - 7.5) * STEP_XY
    level = lax.axis_index(VZ) * PLANES + jnp.arange(PLANES, dtype=jnp.int32)
    vz = ((level.astype(jnp.float32) - 11.5) * STEP_Z)[:, None, None, None]
    flat = (vx - flow_x) ** 2 + (vy - flow_y) ** 2
    return keep * kicked + gain * jnp.exp(cool * (flat + (vz - flow_z) ** 2))


def solution(mesh):
    torus = Mesh(mesh.devices.reshape(mesh.shape["gx"] // 8, 2, 4, 4, 2), AXES)
    return jax.shard_map(
        per_device,
        mesh=torus,
        in_specs=(P(VZ, GX, None, None), P(), P(), P(GX, None), P(GX, None)),
        out_specs=P(VZ, GX, None, None),
        check_vma=False,
    )
```

profile of v0, /device:TPU:1, one launch (start us, length us, event | category | flops | bytes accessed | tf_op | source)
XLA Modules:
  0.0 69.4 jit_solution(17590342253565707529)
XLA Ops:
  0.0 1.7 %shard_map.55 = s32[1]{0:T(128)} custom-call(s32[16]{0:T(128)} %depth.1), custom_call_target="tpu_custom_call" | custom-call | tf_op jit(solution)/shard_map/pallas_call | solution.py:480
  2.4 65.1 %conditional.1 = ((f32[3,8,64,256]{3,2,1,0:T(8,128)S(1)}, f32[6,8,64]{2,1,0:T(8,128)S(1)})) conditional(s32[]{:T(128)} %bitcast, (s32[16]{0:T(128)}, f32[16]{0:T(128)}, f32[8,64]{1,0:T(8,128)}, f32[8,64]{1,0:T(8,128)}, f32[3,8,64,256]{3,2,1,0:T(8,128)}) %tuple.26, (s32[16]{0:T(128)}, f32[16]{0:T(128)}, ...), branch_computations={%region_0.0_spmd, %region_1.0_spmd, %region_2.0_spmd, %region_3.0_... | conditional | bytes 8 | solution.py:483
  2.7 64.5 %branch_3_fun.1 = (f32[3,8,64,256]{3,2,1,0:T(8,128)S(1)}, f32[6,8,64]{2,1,0:T(8,128)S(1)}) custom-call(s32[16]{0:T(128)} %get-tuple-element.90.depth, f32[16]{0:T(128)} %get-tuple-element.91.sub, f32[8,64]{1,0:T(8,128)} %get-tuple-element.92.kick, f32[8,64]{1,0:T(8,128)} %get-tuple-element.93.rate, f32[3,8,64,256]{3,2,1,0:T(8,128)} %get-tuple-element.94.dens), custom_call_target="tpu_custom_call" | custom-call | tf_op jit(solution)/shard_map/cond/branch_3_fun/pallas_call | solution.py:419
  67.5 0.1 subtract_multiply_fusion
  67.6 0.2 multiply_add_fusion.1
  67.8 1.6 %multiply_add_fusion = f32[3,8,64,256]{3,2,1,0:T(8,128)} fusion(f32[3,8,64,256]{3,2,1,0:T(8,128)S(1)} %get-tuple-element.113, f32[3,8,64]{2,1,0:T(8,128)S(1)} %subtract_multiply_fusion, f32[8,64,256]{2,1,0:T(8,128)S(1)} %multiply_add_fusion.1, f32[8,64]{1,0:T(8,128)S(1)} %get-tuple-element.118, f32[8,64]{1,0:T(8,128)S(1)} %get-tuple-element.119, ...), kind=kLoop, calls=%fused_computation | loop fusion | flops 1966080 | bytes 3682304 | tf_op jit(solution)/shard_map/add | solution.py:491
  (3 shorter events, 0.0 us)
where the time goes:
time: 68.1 us; the launch traced here: 69.4 us
  Pallas kernels  66.2 us (97%)
  other arithmetic  1.93 us (3%)
  between operations  0.69 us (1%)
    pallas_call x1, Pallas kernels, step(): pl.pallas_call(functools.partial(kernel, cap), out_shape=(jax.ShapeDtypeS...  64.5 us
    pallas_call x1, Pallas kernels, per_device(): pl.pallas_call(branch_kernel, out_shape=jax.ShapeDtypeStruct((1,), jnp.in...  1.73 us
    add x1, other arithmetic, per_device(): return keep * kicked + gain * jnp.exp(cool * (flat + (vz - flow_z) ** 2))  1.64 us

commit v1 on v0

--- a/solution.py
+++ b/solution.py
@@ -26,7 +26,7 @@
 TILES = QUARTER // TR
 CHUNKS = [(p, t) for p in (0, 2, 1) for t in range(TILES)]
 N = len(CHUNKS)
-LENGTHS = (23, 25, 26, 28, 30, 33, 42)
+LENGTHS = (23, 25, 27, 29, 31, 34, 42)
 REACH = 21
 SPAN = WIDE + 2 * REACH
 
@@ -310,6 +310,10 @@
     down = remote(planes.at[1], planes.at[4], halo_out.at[0], halo_in.at[0], slab_device((slab + slabs - 1) % slabs))
     up = remote(planes.at[3], planes.at[0], halo_out.at[1], halo_in.at[1], slab_device((slab + 1) % slabs))
 
+    a = kick[...]
+    lift, drop, stay = jnp.maximum(a, 0.0), jnp.maximum(-a, 0.0), 1.0 - jnp.abs(a)
+    totals = [jnp.zeros((COLS, ROWS), jnp.float32) for _ in range(5)]
+
     def stage_plane(p):
         for c, (q, _) in enumerate(CHUNKS):
             if q == p:
@@ -335,13 +339,6 @@
         for b in range(2):
             four_cols(b, 0)
 
-    for name, c in ORDER:
-        {"A": stage_pack, "B": stage_forward, "C": stage_merge, "D": stage_plane}[name](c)
-
-    a = kick[...]
-    lift, drop, stay = jnp.maximum(a, 0.0), jnp.maximum(-a, 0.0), 1.0 - jnp.abs(a)
-    totals = [jnp.zeros((COLS, ROWS), jnp.float32) for _ in range(5)]
-    for p in range(PLANES):
         level = slab * PLANES + p
         up_on = jnp.where(level + 1 < TOTAL_VZ, lift, 0.0)
         down_on = jnp.where(level >= 1, drop, 0.0)
@@ -356,6 +353,10 @@
         )
         for j, term in enumerate((n0 * kept, n1 * kept, n2 * kept, n0 * lean, n3 * kept + n0 * heat)):
             totals[j] = totals[j] + term
+
+    for name, c in ORDER:
+        {"A": stage_pack, "B": stage_forward, "C": stage_merge, "D": stage_plane}[name](c)
+
     for j in range(5):
         part[j // 2, :, j % 2 * ROWS : (j % 2 + 1) * ROWS] = totals[j]
 

time: 68.1 us -> 66.7 us (0.979); the launches traced: 69.4 us -> 66.5 us
  Pallas kernels: 66.2 us -> 63.3 us
    pallas_call x1, Pallas kernels: 64.5 us -> 61.6 us  [step(): pl.pallas_call(functools.partial(kernel, cap), out_shape=(jax.ShapeDtypeS...]
where the time goes in v1:
time: 66.7 us; the launch traced here: 66.5 us
  Pallas kernels  63.3 us (95%)
  other arithmetic  1.93 us (3%)
  between operations  0.69 us (1%)
    pallas_call x1, Pallas kernels, step(): pl.pallas_call(functools.partial(kernel, cap), out_shape=(jax.ShapeDtypeS...  61.6 us
    pallas_call x1, Pallas kernels, per_device(): pl.pallas_call(branch_kernel, out_shape=jax.ShapeDtypeStruct((1,), jnp.in...  1.73 us
    add x1, other arithmetic, per_device(): return keep * kicked + gain * jnp.exp(cool * (flat + (vz - flow_z) ** 2))  1.64 us

profile of v1, /device:TPU:1, one launch (start us, length us, event | category | flops | bytes accessed | tf_op | source)
XLA Modules:
  0.0 66.5 jit_solution(15040969863693315290)
XLA Ops:
  0.0 1.7 %shard_map.55 = s32[1]{0:T(128)} custom-call(s32[16]{0:T(128)} %depth.1), custom_call_target="tpu_custom_call" | custom-call | tf_op jit(solution)/shard_map/pallas_call | solution.py:481
  2.4 62.2 %conditional.1 = ((f32[3,8,64,256]{3,2,1,0:T(8,128)S(1)}, f32[6,8,64]{2,1,0:T(8,128)S(1)})) conditional(s32[]{:T(128)} %bitcast, (s32[16]{0:T(128)}, f32[16]{0:T(128)}, f32[8,64]{1,0:T(8,128)}, f32[8,64]{1,0:T(8,128)}, f32[3,8,64,256]{3,2,1,0:T(8,128)}) %tuple.26, (s32[16]{0:T(128)}, f32[16]{0:T(128)}, ...), branch_computations={%region_0.0_spmd, %region_1.0_spmd, %region_2.0_spmd, %region_3.0_... | conditional | bytes 8 | solution.py:484
  2.4 61.6 %branch_1_fun.1 = (f32[3,8,64,256]{3,2,1,0:T(8,128)S(1)}, f32[6,8,64]{2,1,0:T(8,128)S(1)}) custom-call(s32[16]{0:T(128)} %get-tuple-element.80.depth, f32[16]{0:T(128)} %get-tuple-element.81.sub, f32[8,64]{1,0:T(8,128)} %get-tuple-element.82.kick, f32[8,64]{1,0:T(8,128)} %get-tuple-element.83.rate, f32[3,8,64,256]{3,2,1,0:T(8,128)} %get-tuple-element.84.dens), custom_call_target="tpu_custom_call" | custom-call | tf_op jit(solution)/shard_map/cond/branch_1_fun/pallas_call | solution.py:420
  64.6 0.1 subtract_multiply_fusion
  64.7 0.2 multiply_add_fusion.1
  64.9 1.6 %multiply_add_fusion = f32[3,8,64,256]{3,2,1,0:T(8,128)} fusion(f32[3,8,64,256]{3,2,1,0:T(8,128)S(1)} %get-tuple-element.113, f32[3,8,64]{2,1,0:T(8,128)S(1)} %subtract_multiply_fusion, f32[8,64,256]{2,1,0:T(8,128)S(1)} %multiply_add_fusion.1, f32[8,64]{1,0:T(8,128)S(1)} %get-tuple-element.118, f32[8,64]{1,0:T(8,128)S(1)} %get-tuple-element.119, ...), kind=kLoop, calls=%fused_computation | loop fusion | flops 1966080 | bytes 3682304 | tf_op jit(solution)/shard_map/add | solution.py:492
  (3 shorter events, 0.0 us)
